TPU v7x, 256 devices: a whole 4x4x8 slice. The times are simulated.
256 devices in a mesh: rep: 16 (over y, z_lo), fsdp: 16 (over x, z_hi, core).
Axes of the slice: x: 4, y: 4, z: 8 (z_hi: 2, z_lo: 4; z = z_hi * 4 + z_lo), core: 2. Of those that a mesh axis runs over, the one named last changes fastest.
Arguments:
- gradients: bfloat16 [16, 16, 1024, 2048], P('rep', 'fsdp'), may hold values from -6 to 6
- momentum: float32 [16, 1024, 2048], P('rep', None, 'fsdp'), may hold values from -12 to 12
- master_weights: float32 [1024, 2048], P(None, 'fsdp'), may hold values from -0.125 to 0.125
Outputs:
- new_momentum: float32 [16, 1024, 2048], P('rep', None, 'fsdp')
- new_master: float32 [1024, 2048], P(None, 'fsdp')
- weights_full: bfloat16 [1024, 2048], replicated
All inputs are finite; a program needn't handle non-finite values.
Results may differ from a plain program's by a relative error of at most 0.012.
Values may be sent and summed in bfloat16 or wider, within the bound.
No kernel may reach another device: no remote copies, remote signals or barrier semaphores. Data moves between devices by JAX's collectives and lax.ppermute only.
A program may use at most 128 MiB of HBM per device.

v0:
```python
import jax
import jax.numpy as jnp
from jax import lax
from jax.sharding import PartitionSpec as P

GROUP = 128
BAND = 16
momentum_decay = 0.9
step_size = 0.05


def sent_to_all(array, axis):
    devices = lax.axis_size(axis)
    return lax.all_to_all(
        jnp.broadcast_to(array[None], (devices, *array.shape)), axis, 0, 0, tiled=True
    )


def taken_together(array, axis):
    return sent_to_all(array, axis).sum(axis=0)


def joined_along(parts, dim):
    shape = list(parts.shape[1:])
    shape[dim] *= parts.shape[0]
    return jnp.moveaxis(parts, 0, dim).reshape(shape)


def collect(array, axis, dim):
    parts = sent_to_all(array, axis)
    return joined_along(parts, dim)


def cosine_rows():
    freq = jnp.arange(BAND, dtype=jnp.float32)[:, None]
    place = jnp.arange(GROUP, dtype=jnp.float32)[None, :]
    factor = jnp.where(freq == 0.0, jnp.sqrt(1.0 / GROUP), jnp.sqrt(2.0 / GROUP)).astype(
        jnp.float32
    )
    return factor * jnp.cos(jnp.pi * (2.0 * place + 1.0) * freq / (2.0 * GROUP))


def band_of(matrix):
    table = cosine_rows()
    blocks = matrix.reshape(matrix.shape[0] // GROUP, GROUP, matrix.shape[1] // GROUP, GROUP)
    return jnp.einsum("kr,arbc,lc->abkl", table, blocks, table)


def spread_band(coeffs):
    table = cosine_rows()
    blocks = jnp.einsum("kr,abkl,lc->arbc", table, coeffs, table)
    return blocks.reshape(coeffs.shape[0] * GROUP, coeffs.shape[1] * GROUP)


def local(gradients, momentum, master_weights):
    prior_full = lax.all_gather(
        master_weights.astype(jnp.bfloat16), "fsdp", axis=1, tiled=True
    ).astype(master_weights.dtype)
    summed = lax.psum_scatter(
        gradients[0, 0].astype(jnp.float32).astype(jnp.bfloat16),
        "fsdp",
        scatter_dimension=1,
        tiled=True,
    ).astype(jnp.float32)
    moment = momentum_decay * momentum[0] + summed
    own_band = band_of(moment)
    remaining = moment - spread_band(own_band)
    mean_band = taken_together(own_band, "rep") / lax.axis_size("rep")
    band_table = collect(mean_band, "fsdp", 1)
    updated_full = prior_full - step_size * spread_band(band_table)
    shard_width = master_weights.shape[1]
    first_column = lax.axis_index("fsdp") * shard_width
    new_master = lax.dynamic_slice_in_dim(updated_full, first_column, shard_width, 1)
    weights_full = updated_full.astype(jnp.bfloat16)
    return (remaining[None], new_master, weights_full)


def solution(mesh):
    return jax.shard_map(
        local,
        mesh=mesh,
        in_specs=(P("rep", "fsdp", None, None), P("rep", None, "fsdp"), P(None, "fsdp")),
        out_specs=(P("rep", None, "fsdp"), P(None, "fsdp"), P()),
        check_vma=False,
    )
```

profile of v0, /device:TPU:1, one launch (start us, length us, event | category | flops | bytes accessed | tf_op | source)
XLA Modules:
  0.0 222.4 jit_solution(7198266306413594838)
XLA Ops:
  7.2 0.0 copy-start
  7.2 0.0 copy-start.1
  7.2 0.0 reduce-scatter.4.cloned.1.call-start
  7.2 6.5 %copy.24 = bf16[1024,2048]{0,1:T(8,128)(2,1)} copy(bf16[1024,2048]{1,0:T(8,128)(2,1)} %bitcast.51) | data formatting | bytes 8388608
  13.7 0.0 reduce-scatter.4.cloned.1.call-update
  13.7 0.0 all-gather.2.cloned.1.call-start
  13.8 0.0 copy-done
  13.8 0.7 convert_element_type.15
  14.5 0.0 all-gather.2.cloned.1.call-update
  14.6 105.9 %reduce-scatter.4.cloned.1.call-done = bf16[128,1024]{1,0:T(8,128)(2,1)} async-done(((bf16[2048,1024]{1,0:T(8,128)(2,1)}), bf16[128,1024]{1,0:T(8,128)(2,1)}) %reduce-scatter.4.cloned.1.call-update) | async-done | bytes 262160
  120.5 1.1 copy.25
  121.6 0.0 copy-done.1
  121.7 0.1 bitcast_add_fusion
  121.7 0.3 fusion.3
  122.0 0.1 broadcast_in_dim.36
  122.1 1.0 reshape.66
  123.2 4.6 %all-to-all-start = ((f32[16,1,2048]{2,1,0:T(1,128)}), f32[16,1,2048]{2,1,0:T(1,128)S(1)}, u32[]{:S(2)}, u32[]{:S(2)}) async-start(f32[16,1,2048]{2,1,0:T(1,128)} %reshape.66), calls=%async_computation | async-start | bytes 262144 | tf_op jit(solution)/shard_map/all_to_all | solution.py:14
  127.8 0.2 convolution_bitcast_fusion
  128.0 7.1 %all-to-all-done = f32[16,1,2048]{2,1,0:T(1,128)S(1)} async-done(((f32[16,1,2048]{2,1,0:T(1,128)}), f32[16,1,2048]{2,1,0:T(1,128)S(1)}, u32[]{:S(2)}, u32[]{:S(2)}) %all-to-all-start) | async-done | bytes 131104 | tf_op jit(solution)/shard_map/all_to_all | solution.py:14
  135.1 0.5 broadcast.93
  135.6 0.9 reduce.1
  136.6 0.4 reshape.67
  136.9 0.1 reduce_sum.9
  137.0 0.1 copy.19
  137.1 0.1 broadcast_bitcast_fusion
  137.2 1.2 reshape.68
  138.4 8.8 %all-to-all-start.1 = ((bf16[16,2,1024]{2,1,0:T(2,128)(2,1)}), bf16[16,2,1024]{2,1,0:T(2,128)(2,1)S(1)}, u32[]{:S(2)}, u32[]{:S(2)}) async-start(bf16[16,2,1024]{2,1,0:T(2,128)(2,1)} %reshape.68), calls=%async_computation.1 | async-start | bytes 131072 | tf_op jit(solution)/shard_map/all_to_all | solution.py:14
  147.2 1.1 fusion.2
  148.3 8.7 %all-to-all-done.1 = bf16[16,2,1024]{2,1,0:T(2,128)(2,1)S(1)} async-done(((bf16[16,2,1024]{2,1,0:T(2,128)(2,1)}), bf16[16,2,1024]{2,1,0:T(2,128)(2,1)S(1)}, u32[]{:S(2)}, u32[]{:S(2)}) %all-to-all-start.1) | async-done | bytes 65568 | tf_op jit(solution)/shard_map/all_to_all | solution.py:14
  157.0 0.4 reshape.69
  157.3 4.3 %multiply_bitcast_fusion = f32[8,128,16,128]{3,1,2,0:T(8,128)} fusion(f32[128]{0:T(128)S(1)} %add_multiply_fusion, f32[16]{0:T(128)S(1)} %compare_select_fusion, bf16[16,1,8,16,16]{4,3,2,1,0:T(8,128)(2,1)S(1)} %reshape.69), kind=kOutput, calls=%fused_computation.1 | convolution fusion | flops 77606912 | bytes 8454720 | tf_op jit(solution)/shard_map/kr,abkl,lc->arbc/dot_general | solution.py:51
  161.7 11.3 %copy.21 = f32[8,128,16,128]{3,2,1,0:T(8,128)} copy(f32[8,128,16,128]{3,1,2,0:T(8,128)} %multiply_bitcast_fusion) | data formatting | bytes 16777216 | tf_op jit(solution)/shard_map/mul | solution.py:70
  173.0 26.6 %all-gather.2.cloned.1.call-done = bf16[1024,2048]{1,0:T(8,128)(2,1)} async-done(((bf16[1024,128]{1,0:T(8,128)(2,1)}), bf16[1024,2048]{1,0:T(8,128)(2,1)}) %all-gather.2.cloned.1.call-update) | async-done | bytes 4194320 | tf_op jit(solution)/shard_map/all_gather | solution.py:56
  199.6 14.1 %fusion.41 = (bf16[1024,2048]{1,0:T(8,128)(2,1)}, f32[1024,2048]{1,0:T(8,128)}) fusion(f32[128,8,16,128]{3,2,1,0:T(8,128)} %bitcast.48, bf16[1024,2048]{1,0:T(8,128)(2,1)} %all-gather.2.cloned.1.call-done), kind=kLoop, calls=%fused_computation.37 | loop fusion | flops 6291456 | bytes 25165824 | tf_op jit(solution)/shard_map/convert_element_type | solution.py:74
  213.7 1.9 constant_dynamic-slice_fusion
  (3 shorter events, 0.0 us)
Async XLA Ops:
  7.2 6.6 %copy-start = (f32[1024,128]{1,0:T(8,128)S(1)}, f32[1024,128]{1,0:T(8,128)}, u32[]{:S(2)}) copy-start(f32[1024,128]{1,0:T(8,128)} %param.5) | copy-start | bytes 1572868
  7.2 114.5 %copy-start.1 = (f32[1,1024,128]{2,1,0:T(8,128)S(1)}, f32[1,1024,128]{2,1,0:T(8,128)}, u32[]{:S(2)}) copy-start(f32[1,1024,128]{2,1,0:T(8,128)} %param.4) | copy-start | bytes 1572868
  7.2 113.3 %reduce-scatter.4.cloned.1.call-start = ((), (), s32[]{:S(2)}) async-start(), calls=%async_computation.4 | async-start | bytes 4456448
  13.7 185.9 %all-gather.2.cloned.1.call-start = ((), (), s32[]{:S(2)}) async-start(), calls=%async_computation.3 | async-start | bytes 4456448 | tf_op jit(solution)/shard_map/all_gather | solution.py:56
  123.2 11.9 %all-to-all-start = ((f32[16,1,2048]{2,1,0:T(1,128)}), f32[16,1,2048]{2,1,0:T(1,128)S(1)}, u32[]{:S(2)}, u32[]{:S(2)}) async-start(f32[16,1,2048]{2,1,0:T(1,128)} %reshape.66), calls=%async_computation | async-start | bytes 262144 | tf_op jit(solution)/shard_map/all_to_all | solution.py:14
  138.4 18.5 %all-to-all-start.1 = ((bf16[16,2,1024]{2,1,0:T(2,128)(2,1)}), bf16[16,2,1024]{2,1,0:T(2,128)(2,1)S(1)}, u32[]{:S(2)}, u32[]{:S(2)}) async-start(bf16[16,2,1024]{2,1,0:T(2,128)(2,1)} %reshape.68), calls=%async_computation.1 | async-start | bytes 131072 | tf_op jit(solution)/shard_map/all_to_all | solution.py:14
Sparse Core Ops, SparseCore 0:
  13.9 106.6 reduce-scatter.3
  124.0 75.6 all-gather.1
where the time goes:
time: 223 us; the launch traced here: 222 us
  waiting for transfers between devices  148 us (66%)
  local copies, waits for them, and re-layouts  24.6 us (11%)
  other arithmetic  15.9 us (7%)
  between operations  14.2 us (6%)
  starting transfers between devices  13.5 us (6%)
  matrix products  5.91 us (3%)
    unnamed x3, waiting for transfers between devices  106 us
    all_gather x1, waiting for transfers between devices, local(): lax.all_gather(master_weights.astype(jnp.bfloat16), 'fsdp', axis=1, tiled...  26.6 us
    all_to_all x2, waiting for transfers between devices, sent_to_all(): lax.all_to_all(jnp.broadcast_to(array[None], (devices, *array.shape)), ax...  15.8 us
    convert_element_type x1, other arithmetic, local(): weights_full = updated_full.astype(jnp.bfloat16)  14.1 us
    all_to_all x2, starting transfers between devices, sent_to_all(): lax.all_to_all(jnp.broadcast_to(array[None], (devices, *array.shape)), ax...  13.4 us
    mul x1, local copies, waits for them, and re-layouts, local(): updated_full = prior_full - step_size * spread_band(band_table)  11.3 us
    unnamed x11, local copies, waits for them, and re-layouts  10.7 us
    dot_general x3, matrix products, spread_band(): blocks = jnp.einsum('kr,abkl,lc->arbc', table, coeffs, table)  5.6 us
  transfers between devices with their start and end apart: 4, of which 4 were waited for; matrix products, arithmetic and copies ran while one was open for 11% of the time, Pallas kernels for 0%

commit v1 on v0

--- a/solution.py
+++ b/solution.py
@@ -53,8 +53,11 @@
 
 
 def local(gradients, momentum, master_weights):
-    prior_full = lax.all_gather(
-        master_weights.astype(jnp.bfloat16), "fsdp", axis=1, tiled=True
+    prior_full = jnp.concatenate(
+        lax.all_to_all(
+            jnp.stack([master_weights.astype(jnp.bfloat16)] * lax.axis_size("fsdp")), "fsdp", 0, 0
+        ),
+        axis=1,
     ).astype(master_weights.dtype)
     summed = lax.psum_scatter(
         gradients[0, 0].astype(jnp.float32).astype(jnp.bfloat16),

time: 223 us -> 279 us (1.25)
  waiting for transfers between devices: 148 us -> 198 us
  blocking collectives: 0 us -> 11.7 us
  other arithmetic: 15.9 us -> 10.1 us
    all_to_all x0 -> x1, waiting for transfers between devices: none -> 81.3 us  [local(): lax.all_to_all(jnp.stack([master_weights.astype(jnp.bfloat16)] * lax.axis...]
    all_gather x1 -> x0, waiting for transfers between devices: 26.6 us -> none  [local(): lax.all_gather(master_weights.astype(jnp.bfloat16), 'fsdp', axis=1, tiled...]
    all_to_all x0 -> x1, blocking collectives: none -> 11.7 us  [sent_to_all(): lax.all_to_all(jnp.broadcast_to(array[None], (devices, *array.shape)), ax...]
    all_to_all x2 -> x1, waiting for transfers between devices: 15.8 us -> 9.69 us  [sent_to_all(): lax.all_to_all(jnp.broadcast_to(array[None], (devices, *array.shape)), ax...]
    convert_element_type x1, other arithmetic: 14.1 us -> 8.97 us  [local(): weights_full = updated_full.astype(jnp.bfloat16)]
    all_to_all x0 -> x1, starting transfers between devices: none -> 4.71 us  [local(): lax.all_to_all(jnp.stack([master_weights.astype(jnp.bfloat16)] * lax.axis...]
    all_to_all x2 -> x1, starting transfers between devices: 13.4 us -> 8.8 us  [sent_to_all(): lax.all_to_all(jnp.broadcast_to(array[None], (devices, *array.shape)), ax...]
    another operation x0 -> x1, local copies, waits for them, and re-layouts: none -> 2.82 us  [local(): jnp.stack([master_weights.astype(jnp.bfloat16)] * lax.axis_size('fsdp'))]
  transfers between devices with their start and end apart: 4 -> 3, of which waited for: 4 -> 3; matrix products, arithmetic and copies ran while one was open for 11% -> 6% of each run, Pallas kernels for 0% -> 0%
where the time goes in v1:
time: 279 us
  waiting for transfers between devices  198 us (71%)
  local copies, waits for them, and re-layouts  25.7 us (9%)
  between operations  14.1 us (5%)
  starting transfers between devices  13.5 us (5%)
  blocking collectives  11.7 us (4%)
  other arithmetic  10.1 us (4%)
  matrix products  5.88 us (2%)
    unnamed x2, waiting for transfers between devices  107 us
    all_to_all x1, waiting for transfers between devices, local(): lax.all_to_all(jnp.stack([master_weights.astype(jnp.bfloat16)] * lax.axis...  81.3 us
    all_to_all x1, blocking collectives, sent_to_all(): lax.all_to_all(jnp.broadcast_to(array[None], (devices, *array.shape)), ax...  11.7 us
    mul x1, local copies, waits for them, and re-layouts, local(): updated_full = prior_full - step_size * spread_band(band_table)  11.3 us
    unnamed x11, local copies, waits for them, and re-layouts  9.98 us
    all_to_all x1, waiting for transfers between devices, sent_to_all(): lax.all_to_all(jnp.broadcast_to(array[None], (devices, *array.shape)), ax...  9.69 us
    convert_element_type x1, other arithmetic, local(): weights_full = updated_full.astype(jnp.bfloat16)  8.97 us
    all_to_all x1, starting transfers between devices, sent_to_all(): lax.all_to_all(jnp.broadcast_to(array[None], (devices, *array.shape)), ax...  8.8 us
  transfers between devices with their start and end apart: 3, of which 3 were waited for; matrix products, arithmetic and copies ran while one was open for 6% of the time, Pallas kernels for 0%

profile of v1, /device:TPU:1, one launch (start us, length us, event | category | flops | bytes accessed | tf_op | source)
XLA Modules:
  0.0 278.8 jit_solution(3395356053698888336)
XLA Ops:
  7.2 0.0 copy-start.1
  7.2 0.0 reduce-scatter.4.cloned.1.call-start
  7.2 6.4 %copy.27 = bf16[1024,2048]{0,1:T(8,128)(2,1)} copy(bf16[1024,2048]{1,0:T(8,128)(2,1)} %bitcast.58) | data formatting | bytes 8388608
  13.7 0.0 copy-start
  13.7 0.0 reduce-scatter.4.cloned.1.call-update
  13.7 106.8 %reduce-scatter.4.cloned.1.call-done = bf16[128,1024]{1,0:T(8,128)(2,1)} async-done(((bf16[2048,1024]{1,0:T(8,128)(2,1)}), bf16[128,1024]{1,0:T(8,128)(2,1)}) %reduce-scatter.4.cloned.1.call-update) | async-done | bytes 262160
  120.5 1.1 copy.28
  121.6 0.0 copy-done.1
  121.6 0.1 bitcast_add_fusion
  121.7 0.3 fusion.3
  122.0 0.1 broadcast_in_dim.36
  122.1 0.4 reshape.73
  122.5 11.7 %all_to_all.15 = f32[16,1,2048]{2,1,0:T(1,128)S(1)} all-to-all(f32[16,1,2048]{2,1,0:T(1,128)S(1)} %reshape.73), channel_id=1, replica_groups=mesh['rep'=16,'fsdp'=16] {'rep'}, dimensions={0} | all-to-all | bytes 262144 | tf_op jit(solution)/shard_map/all_to_all | solution.py:14
  134.2 0.5 broadcast.95
  134.7 0.9 reduce.1
  135.7 0.4 reshape.74
  136.0 0.1 reduce_sum.9
  136.1 0.1 copy.22
  136.2 0.1 broadcast_bitcast_fusion
  136.3 1.2 reshape.75
  137.5 8.8 %all-to-all-start.2 = ((bf16[16,2,1024]{2,1,0:T(2,128)(2,1)}), bf16[16,2,1024]{2,1,0:T(2,128)(2,1)S(1)}, u32[]{:S(2)}, u32[]{:S(2)}) async-start(bf16[16,2,1024]{2,1,0:T(2,128)(2,1)} %reshape.75), calls=%async_computation.2 | async-start | bytes 131072 | tf_op jit(solution)/shard_map/all_to_all | solution.py:14
  146.3 0.0 copy-done
  146.4 9.7 %all-to-all-done.2 = bf16[16,2,1024]{2,1,0:T(2,128)(2,1)S(1)} async-done(((bf16[16,2,1024]{2,1,0:T(2,128)(2,1)}), bf16[16,2,1024]{2,1,0:T(2,128)(2,1)S(1)}, u32[]{:S(2)}, u32[]{:S(2)}) %all-to-all-start.2) | async-done | bytes 65568 | tf_op jit(solution)/shard_map/all_to_all | solution.py:14
  156.1 2.8 %stack.2 = bf16[16,1024,128]{2,1,0:T(8,128)(2,1)} broadcast(bf16[1024,128]{1,0:T(8,128)(2,1)S(1)} %convert_element_type.21), dimensions={1,2} | broadcast | bytes 4456448 | tf_op jit(solution)/shard_map/stack | solution.py:58
  158.9 4.7 %all-to-all-start = ((bf16[16,1024,128]{2,1,0:T(8,128)(2,1)}), bf16[16,1024,128]{2,1,0:T(8,128)(2,1)}, u32[]{:S(2)}, u32[]{:S(2)}) async-start(bf16[16,1024,128]{2,1,0:T(8,128)(2,1)} %stack.2), calls=%async_computation | async-start | bytes 8388608 | tf_op jit(solution)/shard_map/all_to_all | solution.py:57
  163.6 0.2 convolution_bitcast_fusion
  163.8 1.1 fusion.2
  164.9 0.4 reshape.76
  165.2 4.3 %multiply_bitcast_fusion = f32[8,128,16,128]{3,1,2,0:T(8,128)} fusion(f32[128]{0:T(128)S(1)} %add_multiply_fusion, f32[16]{0:T(128)S(1)} %compare_select_fusion, bf16[16,1,8,16,16]{4,3,2,1,0:T(8,128)(2,1)S(1)} %reshape.76), kind=kOutput, calls=%fused_computation.2 | convolution fusion | flops 77606912 | bytes 8454720 | tf_op jit(solution)/shard_map/kr,abkl,lc->arbc/dot_general | solution.py:51
  169.5 11.3 %copy.24 = f32[8,128,16,128]{3,2,1,0:T(8,128)} copy(f32[8,128,16,128]{3,1,2,0:T(8,128)} %multiply_bitcast_fusion) | data formatting | bytes 16777216 | tf_op jit(solution)/shard_map/mul | solution.py:73
  180.9 81.3 %all-to-all-done = bf16[16,1024,128]{2,1,0:T(8,128)(2,1)} async-done(((bf16[16,1024,128]{2,1,0:T(8,128)(2,1)}), bf16[16,1024,128]{2,1,0:T(8,128)(2,1)}, u32[]{:S(2)}, u32[]{:S(2)}) %all-to-all-start) | async-done | bytes 4194336 | tf_op jit(solution)/shard_map/all_to_all | solution.py:57
  262.1 9.0 %fusion.41 = (bf16[1024,2048]{1,0:T(8,128)(2,1)}, f32[1024,2048]{1,0:T(8,128)S(1)}) fusion(f32[128,8,16,128]{3,2,1,0:T(8,128)} %bitcast.55, bf16[16,1024,128]{2,1,0:T(8,128)(2,1)} %all-to-all-done), kind=kLoop, calls=%fused_computation.38 | loop fusion | flops 6291456 | bytes 25165824 | tf_op jit(solution)/shard_map/convert_element_type | solution.py:77
  271.1 0.9 constant_dynamic-slice_fusion
  (4 shorter events, 0.1 us)
Async XLA Ops:
  7.2 114.4 %copy-start.1 = (f32[1,1024,128]{2,1,0:T(8,128)S(1)}, f32[1,1024,128]{2,1,0:T(8,128)}, u32[]{:S(2)}) copy-start(f32[1,1024,128]{2,1,0:T(8,128)} %param.4) | copy-start | bytes 1572868
  7.2 113.3 %reduce-scatter.4.cloned.1.call-start = ((), (), s32[]{:S(2)}) async-start(), calls=%async_computation.4 | async-start | bytes 4456448
  13.7 132.7 %copy-start = (f32[1024,128]{1,0:T(8,128)S(1)}, f32[1024,128]{1,0:T(8,128)}, u32[]{:S(2)}) copy-start(f32[1024,128]{1,0:T(8,128)} %param.5) | copy-start | bytes 1572868
  137.5 18.5 %all-to-all-start.2 = ((bf16[16,2,1024]{2,1,0:T(2,128)(2,1)}), bf16[16,2,1024]{2,1,0:T(2,128)(2,1)S(1)}, u32[]{:S(2)}, u32[]{:S(2)}) async-start(bf16[16,2,1024]{2,1,0:T(2,128)(2,1)} %reshape.75), calls=%async_computation.2 | async-start | bytes 131072 | tf_op jit(solution)/shard_map/all_to_all | solution.py:14
  158.9 103.2 %all-to-all-start = ((bf16[16,1024,128]{2,1,0:T(8,128)(2,1)}), bf16[16,1024,128]{2,1,0:T(8,128)(2,1)}, u32[]{:S(2)}, u32[]{:S(2)}) async-start(bf16[16,1024,128]{2,1,0:T(8,128)(2,1)} %stack.2), calls=%async_computation | async-start | bytes 8388608 | tf_op jit(solution)/shard_map/all_to_all | solution.py:57
Sparse Core Ops, SparseCore 0:
  13.8 106.6 reduce-scatter.3
